TPU v7x, 768 devices: a whole 4x8x12 slice. The times are simulated.
768 devices in a mesh: dom: 96 (over z, y_hi, core), sub: 8 (over y_lo, x).
Axes of the slice: x: 4, y: 8 (y_hi: 4, y_lo: 2; y = y_hi * 2 + y_lo), z: 12, core: 2. Of those that a mesh axis runs over, the one named last changes fastest.
Arguments:
- modal_state: float32 [56, 9, 98304], P(None, None, ('dom', 'sub')), may hold values from -6 to 6
- stiffness: float32 [3, 56, 56], replicated, may hold values from -0.75 to 0.75
- jacobians: float32 [3, 9, 9, 98304], P(None, None, None, ('dom', 'sub')), may hold values from -1.25 to 1.25
- flux_solvers: float32 [2, 4, 9, 9, 98304], P(None, None, None, None, ('dom', 'sub')), may hold values from -0.75 to 0.75
- projector: float32 [4, 21, 56], replicated, may hold values from -0.75 to 0.75
- rotations: float32 [3, 21, 21], replicated, may hold values from -1.25 to 1.25
- yield_stress: float32 [98304], P(('dom', 'sub')), may hold values from 0.5 to 8
- cluster: int32 [98304], P(('dom', 'sub')), may hold values from 0 to 1
- orient: int32 [4, 98304], P(None, ('dom', 'sub')), may hold values from 0 to 2
- neighbour_slot: int32 [4, 98304], P(None, ('dom', 'sub')), may hold values from 0 to 703, as said below
- send_map: int32 [147456], P(('dom', 'sub')), may hold values from 0 to 511, as said below
Outputs:
- updated: float32 [56, 9, 98304], P(None, None, ('dom', 'sub'))
Inputs may be any that keep to these rules, and one draw needn't show every extreme that they name: `neighbour_slot`: within one partition every received slot 512 + r is named by exactly one face; the other faces name local faces. `send_map`: the 192 entries of one partition are distinct local face numbers.
All inputs are finite; a program needn't handle non-finite values.
Results may differ from a plain program's by a relative error of at most 0.0003.
Values sent between devices are 32-bit elements; how exact they have to be, the bound alone decides.
A program may use at most 64 MiB of HBM per device.

v0:
```python
import math

import jax
import jax.numpy as jnp
from jax import lax
from jax.experimental import pallas as pl
from jax.experimental.pallas import tpu as pltpu
from jax.sharding import PartitionSpec as P

ORDER = 6
NB = 56
NQ = 9
NM = 21
MP = 24
NF = 4
NE = 128
SLOTS_DOM = 64
SLOTS_SUB = 32
ROWS = NQ * MP
LANES = NF * NE
HALF = 112
QUARTER = 64
MESH = pl.DeviceIdType.MESH
F32 = jnp.float32
BF16 = jnp.bfloat16


def dot(a, b):
    return jnp.dot(a, b, preferred_element_type=F32)


def dot_t(a, b):
    return lax.dot_general(a, b, (((0,), (0,)), ((), ())), preferred_element_type=F32)


def halves(x):
    high = x.astype(BF16).astype(F32)
    return high, x - high


def split_rows(x):
    high, low = halves(x)
    return jnp.concatenate([high, low, high], axis=0).astype(BF16)


def iota(shape, dim):
    return lax.broadcasted_iota(jnp.int32, shape, dim)


def as_bf16(mask):
    return jnp.where(mask, 1.0, 0.0).astype(BF16)


def split_weights(w):
    k = w.shape[1]
    high, low = halves(w)
    row, col = iota((k, 3 * k), 0), iota((k, 3 * k), 1)
    twice = as_bf16((col == row) | (col == row + k))
    once = as_bf16(col == row + 2 * k)
    return (dot(high.astype(BF16), twice) + dot(low.astype(BF16), once)).astype(BF16)


def split_weights_t(w):
    k = w.shape[0]
    high, low = halves(w)
    row, col = iota((k, 3 * k), 0), iota((k, 3 * k), 1)
    twice = as_bf16((col == row) | (col == row + k))
    once = as_bf16(col == row + 2 * k)
    return (dot_t(high.astype(BF16), twice) + dot_t(low.astype(BF16), once)).astype(BF16)


def split_lift(w):
    high, low = halves(w)
    rows, cols = NF * MP, 3 * NF * MP
    row, col = iota((rows, cols), 0), iota((rows, cols), 1)
    face = (
        (row >= MP).astype(jnp.int32)
        + (row >= 2 * MP).astype(jnp.int32)
        + (row >= 3 * MP).astype(jnp.int32)
    )
    start = row + 2 * MP * face
    twice = as_bf16((col == start) | (col == start + MP))
    once = as_bf16(col == start + 2 * MP)
    return (dot_t(high.astype(BF16), twice) + dot_t(low.astype(BF16), once)).astype(BF16)


def tiles(x):
    return x.reshape(x.shape[0] // 8, 8, x.shape[1])


def flat(x):
    return x.reshape(x.shape[0] * 8, x.shape[2])


def by_power(step, values):
    chosen = jnp.float32(values[-1])
    for index in range(len(values) - 2, -1, -1):
        chosen = jnp.where(step == index, jnp.float32(values[index]), chosen)
    return chosen


def prepare_weights(stiff, proj, rot, w_der, w_vol, w_proj, w_lift, w_rot, padded, padded_rot):
    for d in range(3):
        s = stiff[d]
        w_der[d * NB : (d + 1) * NB, :] = split_weights(s)
        w_vol[d * NB : (d + 1) * NB, :] = split_weights_t(s)
    padded[...] = jnp.zeros_like(padded)
    for m in range(NM):
        for f in range(NF):
            padded[f * MP + m : f * MP + m + 1, :] = proj[m, f : f + 1, :]
    w_proj[...] = split_weights(padded[...])
    w_lift[...] = split_lift(padded[...])
    padded_rot[...] = jnp.zeros_like(padded_rot)
    for o in range(3):
        padded_rot[o * MP : o * MP + NM, 0:NM] = rot[o]
    w_rot[...] = split_weights(padded_rot[...])


def spread_rows(jac, flux, jac_wide, flux_wide):
    for q in range(NQ):
        for p in range(NQ):
            for d in range(3):
                jac_wide[(q * NQ + p) * 3 + d] = jnp.broadcast_to(jac[q, p, d : d + 1, :], (8, NE))
            for s in range(2):
                for f in range(NF):
                    flux_wide[((s * NF + f) * NQ + q) * NQ + p] = jnp.broadcast_to(
                        flux[s, q, p, f : f + 1, :], (8, NE)
                    )


def pick_tables(slot, send_map, spare, picks, packs):
    for f in range(NF):
        want = slot[f : f + 1, :]
        rows = picks.shape[0]
        picks[:, f * NE : (f + 1) * NE] = as_bf16(
            iota((rows, NE), 0) == jnp.broadcast_to(want, (rows, NE))
        )
    lane = iota((8, NE), 1)
    first = jnp.broadcast_to(send_map[0:1, 0:NE], (8, NE))
    turned = pltpu.roll(first, 64, 1)
    spare[:, 0:64] = jnp.broadcast_to(send_map[0:1, NE : NE + 64], (8, 64))
    second = spare[...]
    by = [second] + [pltpu.roll(second, 32 * r, 1) for r in (1, 2, 3)]
    group = (
        (lane >= 32).astype(jnp.int32)
        + (lane >= 64).astype(jnp.int32)
        + (lane >= 96).astype(jnp.int32)
    )

    def four(a, b, c, d):
        return jnp.where(
            group == 0, a, jnp.where(group == 1, b, jnp.where(group == 2, c, d))
        )

    wants = [
        jnp.where(lane < 64, first, turned),
        jnp.where(lane < 64, turned, first),
        four(by[0], by[1], by[2], by[3]),
        four(by[3], by[0], by[1], by[2]),
    ]
    for t in range(4):
        packs[:, t * NE : (t + 1) * NE] = as_bf16(
            iota((LANES, NE), 0) == jnp.broadcast_to(wants[t][0:1, :], (LANES, NE))
        )


def apply_stiffness(weights, fields, out, start, count):
    rhs = jnp.concatenate([split_rows(fields[i]) for i in range(count)], axis=1)
    out[:, start * NE : (start + count) * NE] = dot(weights[...], rhs)


def mix(mats, jac_wide, block):
    totals = [None] * len(block)
    for q in range(NQ):
        for d in range(3):
            t = tiles(mats[d * NB : (d + 1) * NB, q * NE : (q + 1) * NE])
            for i, p in enumerate(block):
                term = t * jac_wide[(q * NQ + p) * 3 + d][None]
                totals[i] = term if totals[i] is None else totals[i] + term
    return [flat(t) for t in totals]


BLOCKS = ((0, 1, 2), (3, 4, 5), (6, 7, 8))


def predict(state, w_der, jac_wide, mats, one, two):
    ones = [1.0 / math.factorial(k + 1) for k in range(ORDER)]
    twos = [(2.0 ** (k + 1) - 1.0) / math.factorial(k + 1) for k in range(ORDER)]
    for block in BLOCKS:
        fields = [state[p] for p in block]
        for p, x in zip(block, fields):
            one[p] = x
            if two is not None:
                two[p] = x
        apply_stiffness(w_der, fields, mats[0], block[0], 3)

    def advance(source, target, c1, c2):
        for block in BLOCKS:
            fields = mix(source, jac_wide, block)
            for p, x in zip(block, fields):
                one[p] = one[p] + c1 * x
                if two is not None:
                    two[p] = two[p] + c2 * x
            if target is not None:
                apply_stiffness(w_der, fields, target, block[0], 3)

    def pair(step, carry):
        advance(mats[0], mats[1], by_power(step, ones[1::2][:2]), by_power(step, twos[1::2][:2]))
        advance(mats[1], mats[0], by_power(step, ones[2::2][:2]), by_power(step, twos[2::2][:2]))
        return carry

    lax.fori_loop(0, 2, pair, 0)
    advance(mats[0], None, ones[5], twos[5])


def project(field, w_proj, table):
    for block in BLOCKS:
        rhs = jnp.concatenate([split_rows(field(p)) for p in block], axis=1)
        faces = dot(w_proj[...], rhs)
        for i, p in enumerate(block):
            for f in range(NF):
                table[p * MP : (p + 1) * MP, f * NE : (f + 1) * NE] = faces[
                    f * MP : (f + 1) * MP, i * NE : (i + 1) * NE
                ]


def pick_local(table, picks, packs, packed, picked):
    high, low = halves(table[...])
    both = jnp.concatenate([high, low], axis=0).astype(BF16)
    got = dot(both, packs[...])
    rows = got[0:ROWS] + got[ROWS : 2 * ROWS]
    lane = iota((HALF, NE), 1)
    zeros = jnp.zeros((256 - ROWS, LANES), F32)
    rows = jnp.concatenate([rows, zeros], axis=0)
    for t in range(2):
        cols = slice(t * NE, (t + 1) * NE)
        packed[t][...] = jnp.where(lane < 64, rows[0:HALF, cols], rows[HALF : 2 * HALF, cols])
    lane = iota((QUARTER, NE), 1)
    for t in range(2, 4):
        cols = slice(t * NE, (t + 1) * NE)
        g = [rows[QUARTER * k : QUARTER * (k + 1), cols] for k in range(4)]
        packed[t][...] = jnp.where(
            lane < 64, jnp.where(lane < 32, g[0], g[1]), jnp.where(lane < 96, g[2], g[3])
        )
    return both


def pick_far(got, picks, picked):
    near_low, near_high, side_low, side_high = [g[...] for g in got]
    lane = iota((HALF, NE), 1)
    top = jnp.where(lane < 64, near_low, pltpu.roll(near_high, 64, 1))
    bottom = jnp.where(lane < 64, pltpu.roll(near_low, 64, 1), near_high)
    dom = jnp.concatenate([top, bottom], axis=0)[0:ROWS]
    lane = iota((QUARTER, NE), 1)
    parts = []
    for k in range(4):
        a = side_low if k == 0 else pltpu.roll(side_low, (128 - 32 * k) % 128, 1)
        b = side_high if k == 1 else pltpu.roll(side_high, (160 - 32 * k) % 128, 1)
        parts.append(jnp.where(lane < 32, a, b))
    sub = jnp.concatenate(parts, axis=0)[0:ROWS]
    far = jnp.concatenate([dom, sub], axis=1)
    high, low = halves(far)
    both = jnp.concatenate([high, low], axis=0).astype(BF16)
    picked[...] = picked[...] + dot(both, picks[LANES : LANES + 2 * NE, :])


def turn(picked, w_rot, orient, q):
    high = picked[q * MP : (q + 1) * MP, :]
    low = picked[ROWS + q * MP : ROWS + (q + 1) * MP, :]
    rhs = jnp.concatenate([high, low, high], axis=0).astype(BF16)
    turned = dot(w_rot[...], rhs)
    out = []
    for f in range(NF):
        which = jnp.broadcast_to(orient[f : f + 1, :], (MP, NE))
        c = slice(f * NE, (f + 1) * NE)
        out.append(
            jnp.where(
                which == 0,
                turned[0:MP, c],
                jnp.where(which == 1, turned[MP : 2 * MP, c], turned[2 * MP : 3 * MP, c]),
            )
        )
    return out


def flux_term(face, flux_wide, side, f, total):
    totals = total
    for q in range(NQ):
        x = tiles(face(q))
        new = []
        for p in range(NQ):
            term = x * flux_wide[((side * NF + f) * NQ + q) * NQ + p][None]
            new.append(term if totals is None else totals[p] + term)
        totals = new
    return totals


def kernel(
    state,
    stiff,
    jac,
    flux,
    proj,
    rot,
    stress,
    cluster,
    orient,
    slot,
    send_map,
    out,
    w_der,
    w_vol,
    w_proj,
    w_lift,
    w_rot,
    padded,
    padded_rot,
    jac_wide,
    flux_wide,
    spare,
    picks,
    packs,
    mats_a,
    mats_b,
    first,
    second,
    middle,
    fine_first,
    table_one,
    table_two,
    picked,
    near,
    lifts,
    lift_in,
    send_a,
    send_b,
    send_c,
    send_d,
    recv_a,
    recv_b,
    recv_c,
    recv_d,
    send_sem,
    recv_sem,
    n_dom,
    n_sub,
):
    i, j = lax.axis_index("dom"), lax.axis_index("sub")
    links = (
        (i > 0, {"dom": i - 1}, 1),
        (i < n_dom - 1, {"dom": i + 1}, 0),
        (j > 0, {"sub": j - 1}, 3),
        (j < n_sub - 1, {"sub": j + 1}, 2),
    )
    sends = (send_a, send_b, send_c, send_d)
    recvs = (recv_a, recv_b, recv_c, recv_d)
    barrier = pltpu.get_barrier_semaphore()
    for there, device, _ in links:

        @pl.when(there)
        def _():
            pl.semaphore_signal(barrier, inc=1, device_id=device, device_id_type=MESH)

    def copy(stage, t):
        return pltpu.make_async_remote_copy(
            src_ref=sends[t].at[stage],
            dst_ref=recvs[links[t][2]].at[stage],
            send_sem=send_sem.at[stage, t],
            recv_sem=recv_sem.at[stage, links[t][2]],
            device_id=links[t][1],
            device_id_type=MESH,
        )

    def arrival(stage, t):
        return pltpu.make_async_remote_copy(
            src_ref=sends[t].at[stage],
            dst_ref=recvs[t].at[stage],
            send_sem=send_sem.at[stage, t],
            recv_sem=recv_sem.at[stage, t],
            device_id=links[t][1],
            device_id_type=MESH,
        )

    def start(stage):
        for t in range(4):

            @pl.when(links[t][0])
            def _():
                copy(stage, t).start()

    def finish(stage):
        for t in range(4):

            @pl.when(links[t][0])
            def _():
                copy(stage, t).wait_send()
                arrival(stage, t).wait_recv()

    prepare_weights(stiff, proj, rot, w_der, w_vol, w_proj, w_lift, w_rot, padded, padded_rot)
    spread_rows(jac, flux, jac_wide, flux_wide)
    pick_tables(slot, send_map, spare, picks, packs)
    for t in range(4):

        @pl.when(jnp.logical_not(links[t][0]))
        def _():
            recvs[t][...] = jnp.zeros_like(recvs[t])

    mats = (mats_a, mats_b)
    predict(state, w_der, jac_wide, mats, first, second)
    project(lambda p: first[p], w_proj, table_one)
    both = pick_local(table_one, picks, packs, [s.at[0] for s in sends], picked)
    peers = sum(there.astype(jnp.int32) for there, _, _ in links)
    pl.semaphore_wait(barrier, peers)
    start(0)
    picked[...] = dot(both, picks[0:LANES, :])
    fine = jnp.broadcast_to(cluster[...], (NB, NE)) == 0
    fine_face = jnp.broadcast_to(cluster[...], (MP, NE)) == 0

    def volume(field, base, target):
        for block in BLOCKS:
            apply_stiffness(w_vol, [field(p) for p in block], mats_a, block[0], 3)
        for block in BLOCKS:
            for p, x in zip(block, mix(mats_a, jac_wide, block)):
                target[p] = base(p) + x

    def own_flux(face):
        for f in range(NF):
            totals = flux_term(lambda q: face(q, f), flux_wide, 0, f, None)
            for p in range(NQ):
                lifts[f * NQ + p] = flat(totals[p])

    def near_flux():
        for f in range(NF):
            totals = flux_term(
                lambda q: near[q, f],
                flux_wide,
                1,
                f,
                [tiles(lifts[f * NQ + p]) for p in range(NQ)],
            )
            for p in range(NQ):
                lift_in[f * 3 * MP : (f + 1) * 3 * MP, p * NE : (p + 1) * NE] = split_rows(
                    flat(totals[p])
                )

    def own_one(q, f):
        return table_one[q * MP : (q + 1) * MP, f * NE : (f + 1) * NE]

    def own_two(q, f):
        late = table_two[q * MP : (q + 1) * MP, f * NE : (f + 1) * NE]
        return jnp.where(fine_face, late, own_one(q, f) + late)

    volume(lambda p: first[p], lambda p: state[p], middle)
    own_flux(own_one)
    finish(0)
    pick_far([r.at[0] for r in recvs], picks, picked)
    for q in range(NQ):
        for f, x in enumerate(turn(picked, w_rot, orient, q)):
            near[q, f] = x
    near_flux()
    lifted = dot(w_lift[...], lift_in[...])
    for p in range(NQ):
        middle[p] = jnp.where(fine, middle[p] - lifted[:, p * NE : (p + 1) * NE], state[p])

    predict(middle, w_der, jac_wide, mats, fine_first, None)
    project(lambda p: jnp.where(fine, fine_first[p], second[p]), w_proj, table_two)
    both = pick_local(table_two, picks, packs, [s.at[1] for s in sends], picked)
    start(1)
    picked[...] = dot(both, picks[0:LANES, :])
    volume(
        lambda p: jnp.where(fine, fine_first[p], first[p] + second[p]),
        lambda p: middle[p],
        middle,
    )
    own_flux(own_two)
    finish(1)
    pick_far([r.at[1] for r in recvs], picks, picked)
    for q in range(NQ):
        for f, x in enumerate(turn(picked, w_rot, orient, q)):
            near[q, f] = jnp.where(fine_face, x, near[q, f] + x)
    near_flux()
    lifted = dot(w_lift[...], lift_in[...])
    stepped = [middle[p] - lifted[:, p * NE : (p + 1) * NE] for p in range(NQ)]
    mean = (stepped[0] + stepped[1] + stepped[2]) / 3.0
    spread = [stepped[p] - mean for p in range(3)]
    lead = [s[0:1] for s in spread] + [stepped[p][0:1] for p in range(3, 6)]
    second_inv = (
        0.5 * (lead[0] * lead[0] + lead[1] * lead[1] + lead[2] * lead[2])
        + lead[3] * lead[3]
        + lead[4] * lead[4]
        + lead[5] * lead[5]
    )
    limit = stress[...]
    scaling = jnp.broadcast_to(limit / jnp.maximum(jnp.sqrt(second_inv), limit), (NB, NE))
    for p in range(3):
        out[p] = mean + scaling * spread[p]
        out[3 + p] = scaling * stepped[3 + p]
        out[6 + p] = stepped[6 + p]


def on_device(n_dom, n_sub, modal_state, stiffness, jacobians, flux_solvers, projector, rotations, yield_stress, cluster, orient, neighbour_slot, send_map):
    vmem = pl.BlockSpec(memory_space=pltpu.VMEM)
    field = pltpu.VMEM((NQ, NB, NE), F32)

    def body(*refs):
        kernel(*refs, n_dom, n_sub)

    result = pl.pallas_call(
        body,
        out_shape=jax.ShapeDtypeStruct((NQ, NB, NE), F32),
        in_specs=[vmem] * 11,
        out_specs=vmem,
        scratch_shapes=[
            pltpu.VMEM((3 * NB, 3 * NB), BF16),
            pltpu.VMEM((3 * NB, 3 * NB), BF16),
            pltpu.VMEM((NF * MP, 3 * NB), BF16),
            pltpu.VMEM((NB, 3 * NF * MP), BF16),
            pltpu.VMEM((3 * MP, 3 * MP), BF16),
            pltpu.VMEM((NF * MP, NB), F32),
            pltpu.VMEM((3 * MP, MP), F32),
            pltpu.VMEM((NQ * NQ * 3, 8, NE), F32),
            pltpu.VMEM((2 * NF * NQ * NQ, 8, NE), F32),
            pltpu.VMEM((8, NE), jnp.int32),
            pltpu.VMEM((LANES + 2 * NE, LANES), BF16),
            pltpu.VMEM((LANES, LANES), BF16),
            pltpu.VMEM((3 * NB, NQ * NE), F32),
            pltpu.VMEM((3 * NB, NQ * NE), F32),
            field,
            field,
            field,
            field,
            pltpu.VMEM((ROWS, LANES), F32),
            pltpu.VMEM((ROWS, LANES), F32),
            pltpu.VMEM((2 * ROWS, LANES), F32),
            pltpu.VMEM((NQ, NF, MP, NE), F32),
            pltpu.VMEM((NF * NQ, MP, NE), F32),
            pltpu.VMEM((3 * NF * MP, NQ * NE), BF16),
            pltpu.VMEM((2, HALF, NE), F32),
            pltpu.VMEM((2, HALF, NE), F32),
            pltpu.VMEM((2, QUARTER, NE), F32),
            pltpu.VMEM((2, QUARTER, NE), F32),
            pltpu.VMEM((2, HALF, NE), F32),
            pltpu.VMEM((2, HALF, NE), F32),
            pltpu.VMEM((2, QUARTER, NE), F32),
            pltpu.VMEM((2, QUARTER, NE), F32),
            pltpu.SemaphoreType.DMA((2, 4)),
            pltpu.SemaphoreType.DMA((2, 4)),
        ],
        compiler_params=pltpu.CompilerParams(
            collective_id=0, has_side_effects=True, vmem_limit_bytes=48 << 20
        ),
    )(
        jnp.transpose(modal_state, (1, 0, 2)),
        stiffness,
        jnp.transpose(jacobians, (1, 2, 0, 3)),
        jnp.transpose(flux_solvers, (0, 2, 3, 1, 4)),
        jnp.transpose(projector, (1, 0, 2)),
        rotations,
        yield_stress.reshape(1, -1),
        cluster.reshape(1, -1),
        orient,
        neighbour_slot,
        send_map.reshape(1, -1),
    )
    return jnp.transpose(result, (1, 0, 2))


def solution(mesh):
    both = ("dom", "sub")
    n_dom, n_sub = mesh.shape["dom"], mesh.shape["sub"]
    placed = (
        P(None, None, both),
        P(),
        P(None, None, None, both),
        P(None, None, None, None, both),
        P(),
        P(),
        P(both),
        P(both),
        P(None, both),
        P(None, both),
        P(both),
    )

    def step(*args):
        return on_device(n_dom, n_sub, *args)

    return jax.shard_map(
        step, mesh=mesh, in_specs=placed, out_specs=P(None, None, both), check_vma=False
    )
```

profile of v0, /device:TPU:4, one launch (start us, length us, event | category | flops | bytes accessed | tf_op | source)
XLA Modules:
  0.0 33.0 jit_solution(14121647406364470960)
XLA Ops:
  0.0 0.0 copy-start.10
  0.0 0.0 copy-start.7
  0.0 0.0 copy-start.6
  0.0 0.0 copy-start.8
  0.0 0.0 copy-start.9
  0.0 0.6 %copy-done.10 = s32[128]{0:T(128)S(1)} copy-done((s32[128]{0:T(128)S(1)}, s32[128]{0:T(128)}, u32[]{:S(2)}) %copy-start.10) | copy-done | bytes 536
  0.7 0.0 copy-done.7
  0.7 0.0 copy-done.6
  0.7 0.0 copy-done.8
  0.7 0.0 copy-done.9
  0.7 0.0 copy-start
  0.7 1.0 %copy-done = f32[2,4,9,9,128]{4,1,3,2,0:T(4,128)S(1)} copy-done((f32[2,4,9,9,128]{4,1,3,2,0:T(4,128)S(1)}, f32[2,4,9,9,128]{4,1,3,2,0:T(4,128)}, u32[]{:S(2)}) %copy-start) | copy-done | bytes 331800
  1.7 0.0 copy-start.1
  1.7 0.9 %copy-done.1 = f32[56,9,128]{2,0,1:T(8,128)S(1)} copy-done((f32[56,9,128]{2,0,1:T(8,128)S(1)}, f32[56,9,128]{2,0,1:T(8,128)}, u32[]{:S(2)}) %copy-start.1) | copy-done | bytes 258072
  2.7 0.0 copy-start.2
  2.7 0.9 %copy-done.2 = f32[3,9,9,128]{3,0,2,1:T(4,128)S(1)} copy-done((f32[3,9,9,128]{3,0,2,1:T(4,128)S(1)}, f32[3,9,9,128]{3,0,2,1:T(4,128)}, u32[]{:S(2)}) %copy-start.2) | copy-done | bytes 124440
  3.6 0.0 copy-start.3
  3.6 0.9 %copy-done.3 = f32[3,56,56]{2,1,0:T(8,128)S(1)} copy-done((f32[3,56,56]{2,1,0:T(8,128)S(1)}, f32[3,56,56]{2,1,0:T(8,128)}, u32[]{:S(2)}) %copy-start.3) | copy-done | bytes 37656
  4.5 0.0 copy-start.4
  4.5 0.8 %copy-done.4 = f32[4,21,56]{2,0,1:T(4,128)S(1)} copy-done((f32[4,21,56]{2,0,1:T(4,128)S(1)}, f32[4,21,56]{2,0,1:T(4,128)}, u32[]{:S(2)}) %copy-start.4) | copy-done | bytes 18840
  5.2 0.0 copy-start.5
  5.2 0.8 %copy-done.5 = f32[3,21,21]{2,1,0:T(8,128)S(1)} copy-done((f32[3,21,21]{2,1,0:T(8,128)S(1)}, f32[3,21,21]{2,1,0:T(8,128)}, u32[]{:S(2)}) %copy-start.5) | copy-done | bytes 5316
  6.0 26.3 %shard_map.109 = f32[9,56,128]{2,1,0:T(8,128)S(1)} custom-call(f32[9,56,128]{2,1,0:T(8,128)S(1)} %bitcast.10, f32[3,56,56]{2,1,0:T(8,128)S(1)} %copy-done.3, f32[9,9,3,128]{3,2,1,0:T(4,128)S(1)} %bitcast.11, f32[2,9,9,4,128]{4,3,2,1,0:T(4,128)S(1)} %bitcast.9, f32[21,4,56]{2,1,0:T(4,128)S(1)} %bitcast.12, f32[3,21,21]{2,1,0:T(8,128)S(1)} %copy-done.5, ...), custom_call_target="tpu_custom_call" | custom-call | tf_op jit(solution)/shard_map/pallas_call | solution.py:508
  32.3 0.7 %copy.13 = f32[56,9,128]{2,0,1:T(8,128)} copy(f32[56,9,128]{2,0,1:T(8,128)S(1)} %bitcast.8) | data formatting | bytes 516096
Async XLA Ops:
  0.0 0.7 %copy-start.10 = (s32[128]{0:T(128)S(1)}, s32[128]{0:T(128)}, u32[]{:S(2)}) copy-start(s32[128]{0:T(128)} %param.18) | copy-start | bytes 1540
  0.0 0.7 %copy-start.7 = (s32[4,128]{1,0:T(4,128)S(1)}, s32[4,128]{1,0:T(4,128)}, u32[]{:S(2)}) copy-start(s32[4,128]{1,0:T(4,128)} %refs_9_.1) | copy-start | bytes 6148
  0.0 0.7 %copy-start.6 = (s32[4,128]{1,0:T(4,128)S(1)}, s32[4,128]{1,0:T(4,128)}, u32[]{:S(2)}) copy-start(s32[4,128]{1,0:T(4,128)} %refs_8_.1) | copy-start | bytes 6148
  0.0 0.7 %copy-start.8 = (s32[192]{0:T(256)S(1)}, s32[192]{0:T(256)}, u32[]{:S(2)}) copy-start(s32[192]{0:T(256)} %param.21) | copy-start | bytes 2308
  0.0 0.7 %copy-start.9 = (f32[128]{0:T(128)S(1)}, f32[128]{0:T(128)}, u32[]{:S(2)}) copy-start(f32[128]{0:T(128)} %param.17) | copy-start | bytes 1540
  0.7 1.0 %copy-start = (f32[2,4,9,9,128]{4,1,3,2,0:T(4,128)S(1)}, f32[2,4,9,9,128]{4,1,3,2,0:T(4,128)}, u32[]{:S(2)}) copy-start(f32[2,4,9,9,128]{4,1,3,2,0:T(4,128)} %param.14) | copy-start | bytes 995332
  1.7 0.9 %copy-start.1 = (f32[56,9,128]{2,0,1:T(8,128)S(1)}, f32[56,9,128]{2,0,1:T(8,128)}, u32[]{:S(2)}) copy-start(f32[56,9,128]{2,0,1:T(8,128)} %param.11) | copy-start | bytes 774148
  2.7 0.9 %copy-start.2 = (f32[3,9,9,128]{3,0,2,1:T(4,128)S(1)}, f32[3,9,9,128]{3,0,2,1:T(4,128)}, u32[]{:S(2)}) copy-start(f32[3,9,9,128]{3,0,2,1:T(4,128)} %param.13) | copy-start | bytes 373252
  3.6 0.9 %copy-start.3 = (f32[3,56,56]{2,1,0:T(8,128)S(1)}, f32[3,56,56]{2,1,0:T(8,128)}, u32[]{:S(2)}) copy-start(f32[3,56,56]{2,1,0:T(8,128)} %refs_1_.1) | copy-start | bytes 112900
  4.5 0.8 %copy-start.4 = (f32[4,21,56]{2,0,1:T(4,128)S(1)}, f32[4,21,56]{2,0,1:T(4,128)}, u32[]{:S(2)}) copy-start(f32[4,21,56]{2,0,1:T(4,128)} %param.15) | copy-start | bytes 56452
  5.2 0.8 %copy-start.5 = (f32[3,21,21]{2,1,0:T(8,128)S(1)}, f32[3,21,21]{2,1,0:T(8,128)}, u32[]{:S(2)}) copy-start(f32[3,21,21]{2,1,0:T(8,128)} %refs_5_.1) | copy-start | bytes 15880
where the time goes:
time: 33.4 us; the launch traced here: 33 us
  Pallas kernels  26.3 us (79%)
  local copies, waits for them, and re-layouts  6.68 us (20%)
    pallas_call x1, Pallas kernels, on_device(): pl.pallas_call(body, out_shape=jax.ShapeDtypeStruct((NQ, NB, NE), F32), i...  26.3 us
    unnamed x23, local copies, waits for them, and re-layouts  6.68 us

commit v1 on v0

--- a/solution.py
+++ b/solution.py
@@ -92,35 +92,41 @@
     return x.reshape(x.shape[0] * 8, x.shape[2])
 
 
-def by_power(step, values):
-    chosen = jnp.float32(values[-1])
-    for index in range(len(values) - 2, -1, -1):
-        chosen = jnp.where(step == index, jnp.float32(values[index]), chosen)
-    return chosen
-
-
-def prepare_weights(stiff, proj, rot, w_der, w_vol, w_proj, w_lift, w_rot, padded, padded_rot):
+def prepare_derive(stiff, w_der):
     for d in range(3):
-        s = stiff[d]
-        w_der[d * NB : (d + 1) * NB, :] = split_weights(s)
-        w_vol[d * NB : (d + 1) * NB, :] = split_weights_t(s)
+        w_der[d * NB : (d + 1) * NB, :] = split_weights(stiff[d])
+
+
+def prepare_volume(stiff, w_vol):
+    for d in range(3):
+        w_vol[d * NB : (d + 1) * NB, :] = split_weights_t(stiff[d])
+
+
+def prepare_faces(proj, w_proj, padded):
     padded[...] = jnp.zeros_like(padded)
     for m in range(NM):
         for f in range(NF):
             padded[f * MP + m : f * MP + m + 1, :] = proj[m, f : f + 1, :]
     w_proj[...] = split_weights(padded[...])
-    w_lift[...] = split_lift(padded[...])
+
+
+def prepare_turn(rot, w_rot, padded_rot):
     padded_rot[...] = jnp.zeros_like(padded_rot)
     for o in range(3):
         padded_rot[o * MP : o * MP + NM, 0:NM] = rot[o]
     w_rot[...] = split_weights(padded_rot[...])
 
 
-def spread_rows(jac, flux, jac_wide, flux_wide):
+def spread_jacobians(jac, jac_wide):
     for q in range(NQ):
         for p in range(NQ):
             for d in range(3):
                 jac_wide[(q * NQ + p) * 3 + d] = jnp.broadcast_to(jac[q, p, d : d + 1, :], (8, NE))
+
+
+def spread_flux(flux, flux_wide):
+    for q in range(NQ):
+        for p in range(NQ):
             for s in range(2):
                 for f in range(NF):
                     flux_wide[((s * NF + f) * NQ + q) * NQ + p] = jnp.broadcast_to(
@@ -128,13 +134,15 @@
                     )
 
 
-def pick_tables(slot, send_map, spare, picks, packs):
+def pick_columns(slot, picks):
+    rows = picks.shape[0]
     for f in range(NF):
-        want = slot[f : f + 1, :]
-        rows = picks.shape[0]
         picks[:, f * NE : (f + 1) * NE] = as_bf16(
-            iota((rows, NE), 0) == jnp.broadcast_to(want, (rows, NE))
-        )
+            iota((rows, NE), 0) == jnp.broadcast_to(slot[f : f + 1, :], (rows, NE))
+        )
+
+
+def pack_columns(send_map, spare, packs):
     lane = iota((8, NE), 1)
     first = jnp.broadcast_to(send_map[0:1, 0:NE], (8, NE))
     turned = pltpu.roll(first, 64, 1)
@@ -180,7 +188,7 @@
     return [flat(t) for t in totals]
 
 
-BLOCKS = ((0, 1, 2), (3, 4, 5), (6, 7, 8))
+BLOCKS = ((0, 1), (2, 3), (4, 5), (6, 7), (8,))
 
 
 def predict(state, w_der, jac_wide, mats, one, two):
@@ -192,7 +200,7 @@
             one[p] = x
             if two is not None:
                 two[p] = x
-        apply_stiffness(w_der, fields, mats[0], block[0], 3)
+        apply_stiffness(w_der, fields, mats[0], block[0], len(block))
 
     def advance(source, target, c1, c2):
         for block in BLOCKS:
@@ -202,14 +210,10 @@
                 if two is not None:
                     two[p] = two[p] + c2 * x
             if target is not None:
-                apply_stiffness(w_der, fields, target, block[0], 3)
-
-    def pair(step, carry):
-        advance(mats[0], mats[1], by_power(step, ones[1::2][:2]), by_power(step, twos[1::2][:2]))
-        advance(mats[1], mats[0], by_power(step, ones[2::2][:2]), by_power(step, twos[2::2][:2]))
-        return carry
-
-    lax.fori_loop(0, 2, pair, 0)
+                apply_stiffness(w_der, fields, target, block[0], len(block))
+
+    for k in range(1, 5):
+        advance(mats[(k + 1) % 2], mats[k % 2], ones[k], twos[k])
     advance(mats[0], None, ones[5], twos[5])
 
 
@@ -296,6 +300,18 @@
 
 
 def kernel(
+    state_hbm,
+    stiff_hbm,
+    jac_hbm,
+    flux_hbm,
+    proj_hbm,
+    rot_hbm,
+    stress_hbm,
+    cluster_hbm,
+    orient_hbm,
+    slot_hbm,
+    send_map_hbm,
+    out,
     state,
     stiff,
     jac,
@@ -307,7 +323,7 @@
     orient,
     slot,
     send_map,
-    out,
+    load_sem,
     w_der,
     w_vol,
     w_proj,
@@ -345,6 +361,26 @@
     n_dom,
     n_sub,
 ):
+    loads = {
+        name: pltpu.make_async_copy(source, target, load_sem.at[index])
+        for index, (name, source, target) in enumerate(
+            (
+                ("stiff", stiff_hbm, stiff),
+                ("state", state_hbm, state),
+                ("jac", jac_hbm, jac),
+                ("proj", proj_hbm, proj),
+                ("send_map", send_map_hbm, send_map),
+                ("flux", flux_hbm, flux),
+                ("slot", slot_hbm, slot),
+                ("rot", rot_hbm, rot),
+                ("orient", orient_hbm, orient),
+                ("cluster", cluster_hbm, cluster),
+                ("stress", stress_hbm, stress),
+            )
+        )
+    }
+    for load in loads.values():
+        load.start()
     i, j = lax.axis_index("dom"), lax.axis_index("sub")
     links = (
         (i > 0, {"dom": i - 1}, 1),
@@ -396,9 +432,10 @@
                 copy(stage, t).wait_send()
                 arrival(stage, t).wait_recv()
 
-    prepare_weights(stiff, proj, rot, w_der, w_vol, w_proj, w_lift, w_rot, padded, padded_rot)
-    spread_rows(jac, flux, jac_wide, flux_wide)
-    pick_tables(slot, send_map, spare, picks, packs)
+    loads["stiff"].wait()
+    prepare_derive(stiff, w_der)
+    loads["jac"].wait()
+    spread_jacobians(jac, jac_wide)
     for t in range(4):
 
         @pl.when(jnp.logical_not(links[t][0]))
@@ -406,19 +443,31 @@
             recvs[t][...] = jnp.zeros_like(recvs[t])
 
     mats = (mats_a, mats_b)
+    loads["state"].wait()
     predict(state, w_der, jac_wide, mats, first, second)
+    loads["proj"].wait()
+    prepare_faces(proj, w_proj, padded)
+    loads["send_map"].wait()
+    pack_columns(send_map, spare, packs)
     project(lambda p: first[p], w_proj, table_one)
     both = pick_local(table_one, picks, packs, [s.at[0] for s in sends], picked)
     peers = sum(there.astype(jnp.int32) for there, _, _ in links)
     pl.semaphore_wait(barrier, peers)
     start(0)
+    for name in ("flux", "slot", "rot", "orient", "cluster", "stress"):
+        loads[name].wait()
+    prepare_volume(stiff, w_vol)
+    pick_columns(slot, picks)
+    spread_flux(flux, flux_wide)
+    w_lift[...] = split_lift(padded[...])
+    prepare_turn(rot, w_rot, padded_rot)
     picked[...] = dot(both, picks[0:LANES, :])
     fine = jnp.broadcast_to(cluster[...], (NB, NE)) == 0
     fine_face = jnp.broadcast_to(cluster[...], (MP, NE)) == 0
 
     def volume(field, base, target):
         for block in BLOCKS:
-            apply_stiffness(w_vol, [field(p) for p in block], mats_a, block[0], 3)
+            apply_stiffness(w_vol, [field(p) for p in block], mats_a, block[0], len(block))
         for block in BLOCKS:
             for p, x in zip(block, mix(mats_a, jac_wide, block)):
                 target[p] = base(p) + x
@@ -500,17 +549,31 @@
 
 def on_device(n_dom, n_sub, modal_state, stiffness, jacobians, flux_solvers, projector, rotations, yield_stress, cluster, orient, neighbour_slot, send_map):
     vmem = pl.BlockSpec(memory_space=pltpu.VMEM)
+    hbm = pl.BlockSpec(memory_space=pltpu.HBM)
     field = pltpu.VMEM((NQ, NB, NE), F32)
 
     def body(*refs):
         kernel(*refs, n_dom, n_sub)
 
+    wide = lambda x: pltpu.with_memory_space_constraint(x, pltpu.HBM)
     result = pl.pallas_call(
         body,
         out_shape=jax.ShapeDtypeStruct((NQ, NB, NE), F32),
-        in_specs=[vmem] * 11,
+        in_specs=[hbm] * 11,
         out_specs=vmem,
         scratch_shapes=[
+            pltpu.VMEM((NQ, NB, NE), F32),
+            pltpu.VMEM((3, NB, NB), F32),
+            pltpu.VMEM((NQ, NQ, 3, NE), F32),
+            pltpu.VMEM((2, NQ, NQ, NF, NE), F32),
+            pltpu.VMEM((NM, NF, NB), F32),
+            pltpu.VMEM((3, NM, NM), F32),
+            pltpu.VMEM((1, NE), F32),
+            pltpu.VMEM((1, NE), jnp.int32),
+            pltpu.VMEM((NF, NE), jnp.int32),
+            pltpu.VMEM((NF, NE), jnp.int32),
+            pltpu.VMEM((1, 2 * SLOTS_DOM + 2 * SLOTS_SUB), jnp.int32),
+            pltpu.SemaphoreType.DMA((11,)),
             pltpu.VMEM((3 * NB, 3 * NB), BF16),
             pltpu.VMEM((3 * NB, 3 * NB), BF16),
             pltpu.VMEM((NF * MP, 3 * NB), BF16),
@@ -549,7 +612,7 @@
         compiler_params=pltpu.CompilerParams(
             collective_id=0, has_side_effects=True, vmem_limit_bytes=48 << 20
         ),
-    )(
+    )(*map(wide, (
         jnp.transpose(modal_state, (1, 0, 2)),
         stiffness,
         jnp.transpose(jacobians, (1, 2, 0, 3)),
@@ -561,7 +624,7 @@
         orient,
         neighbour_slot,
         send_map.reshape(1, -1),
-    )
+    )))
     return jnp.transpose(result, (1, 0, 2))
 
 

time: 33.4 us -> 26.9 us (0.81)
  local copies, waits for them, and re-layouts: 6.68 us -> 0.7 us
    unnamed x23 -> x1, local copies, waits for them, and re-layouts: 6.68 us -> 0.7 us
where the time goes in v1:
time: 26.9 us; the launch traced here: 26.8 us
  Pallas kernels  26.1 us (97%)
  local copies, waits for them, and re-layouts  0.7 us (3%)
    pallas_call x1, Pallas kernels, on_device(): pl.pallas_call(body, out_shape=jax.ShapeDtypeStruct((NQ, NB, NE), F32), i...  26.1 us
    unnamed x1, local copies, waits for them, and re-layouts  0.7 us

profile of v1, /device:TPU:4, one launch (start us, length us, event | category | flops | bytes accessed | tf_op | source)
XLA Modules:
  0.0 26.8 jit_solution(8790021374917627630)
XLA Ops:
  0.0 26.1 %shard_map.109 = f32[9,56,128]{2,1,0:T(8,128)S(1)} custom-call(f32[9,56,128]{2,1,0:T(8,128)} %bitcast.10, f32[3,56,56]{2,1,0:T(8,128)} %refs_1_.1, f32[9,9,3,128]{3,2,1,0:T(4,128)} %bitcast.11, f32[2,9,9,4,128]{4,3,2,1,0:T(4,128)} %bitcast.9, f32[21,4,56]{2,1,0:T(4,128)} %bitcast.12, f32[3,21,21]{2,1,0:T(8,128)} %refs_5_.1, f32[1,128]{1,0:T(1,128)} %bitcast.14, ...), custom_call_target="tpu_custom_call" | custom-call | tf_op jit(solution)/shard_map/pallas_call | solution.py:559
  26.1 0.7 %copy.13 = f32[56,9,128]{2,0,1:T(8,128)} copy(f32[56,9,128]{2,0,1:T(8,128)S(1)} %bitcast.8) | data formatting | bytes 516096

commit v2 on v1

--- a/solution.py
+++ b/solution.py
@@ -33,6 +33,10 @@
     return lax.dot_general(a, b, (((0,), (0,)), ((), ())), preferred_element_type=F32)
 
 
+def dot_rows(a, b):
+    return lax.dot_general(a, b, (((1,), (1,)), ((), ())), preferred_element_type=F32)
+
+
 def halves(x):
     high = x.astype(BF16).astype(F32)
     return high, x - high
@@ -191,41 +195,47 @@
 BLOCKS = ((0, 1), (2, 3), (4, 5), (6, 7), (8,))
 
 
-def predict(state, w_der, jac_wide, mats, one, two):
-    ones = [1.0 / math.factorial(k + 1) for k in range(ORDER)]
-    twos = [(2.0 ** (k + 1) - 1.0) / math.factorial(k + 1) for k in range(ORDER)]
+ONES = [1.0 / math.factorial(k + 1) for k in range(ORDER)]
+TWOS = [(2.0 ** (k + 1) - 1.0) / math.factorial(k + 1) for k in range(ORDER)]
+
+
+def predict(state, w_der, jac_wide, mats, one, kept, done):
     for block in BLOCKS:
         fields = [state[p] for p in block]
         for p, x in zip(block, fields):
             one[p] = x
-            if two is not None:
-                two[p] = x
         apply_stiffness(w_der, fields, mats[0], block[0], len(block))
 
-    def advance(source, target, c1, c2):
+    for k in range(1, ORDER):
+        source, target = mats[(k + 1) % 2], mats[k % 2]
         for block in BLOCKS:
             fields = mix(source, jac_wide, block)
             for p, x in zip(block, fields):
-                one[p] = one[p] + c1 * x
-                if two is not None:
-                    two[p] = two[p] + c2 * x
-            if target is not None:
+                one[p] = one[p] + ONES[k] * x
+                if kept is not None:
+                    kept[k - 1, p] = x
+            if k + 1 < ORDER:
                 apply_stiffness(w_der, fields, target, block[0], len(block))
-
-    for k in range(1, 5):
-        advance(mats[(k + 1) % 2], mats[k % 2], ones[k], twos[k])
-    advance(mats[0], None, ones[5], twos[5])
-
-
-def project(field, w_proj, table):
-    for block in BLOCKS:
-        rhs = jnp.concatenate([split_rows(field(p)) for p in block], axis=1)
-        faces = dot(w_proj[...], rhs)
-        for i, p in enumerate(block):
-            for f in range(NF):
-                table[p * MP : (p + 1) * MP, f * NE : (f + 1) * NE] = faces[
-                    f * MP : (f + 1) * MP, i * NE : (i + 1) * NE
-                ]
+            else:
+                done(block)
+
+
+def later(state, kept, two):
+    for p in range(NQ):
+        total = state[p]
+        for k in range(1, ORDER):
+            total = total + TWOS[k] * kept[k - 1, p]
+        two[p] = total
+
+
+def project(fields, block, w_proj, table):
+    rhs = jnp.concatenate([split_rows(x) for x in fields], axis=1)
+    faces = dot(w_proj[...], rhs)
+    for i, p in enumerate(block):
+        for f in range(NF):
+            table[p * MP : (p + 1) * MP, f * NE : (f + 1) * NE] = faces[
+                f * MP : (f + 1) * MP, i * NE : (i + 1) * NE
+            ]
 
 
 def pick_local(table, picks, packs, packed, picked):
@@ -249,7 +259,7 @@
     return both
 
 
-def pick_far(got, picks, picked):
+def far_rows(got):
     near_low, near_high, side_low, side_high = [g[...] for g in got]
     lane = iota((HALF, NE), 1)
     top = jnp.where(lane < 64, near_low, pltpu.roll(near_high, 64, 1))
@@ -263,9 +273,60 @@
         parts.append(jnp.where(lane < 32, a, b))
     sub = jnp.concatenate(parts, axis=0)[0:ROWS]
     far = jnp.concatenate([dom, sub], axis=1)
-    high, low = halves(far)
+    return halves(far)
+
+
+def prepare_slots(flux, orient, picks, rows, lines, slot_flux, slot_turn):
+    rows[80:88, :] = jnp.zeros((8, LANES), F32)
+    for q in range(NQ):
+        for p in range(NQ):
+            for f in range(NF):
+                rows[q * NQ + p : q * NQ + p + 1, f * NE : (f + 1) * NE] = flux[
+                    1, q, p, f : f + 1, :
+                ]
+    high, low = halves(rows[...])
     both = jnp.concatenate([high, low], axis=0).astype(BF16)
-    picked[...] = picked[...] + dot(both, picks[LANES : LANES + 2 * NE, :])
+    far = picks[LANES : LANES + 2 * NE, :]
+    got = dot_rows(both, far)
+    for index in range(NQ * NQ):
+        line = got[index : index + 1, :] + got[88 + index : 89 + index, :]
+        slot_flux[index] = jnp.broadcast_to(line, (8, 2 * NE))
+    for f in range(NF):
+        lines[:, f * NE : (f + 1) * NE] = jnp.broadcast_to(
+            orient[f : f + 1, :].astype(F32), (8, NE)
+        )
+    slot_turn[...] = dot_rows(lines[...].astype(BF16), far)
+
+
+def far_update(got, w_rot, w_lift, picks, slot_flux, slot_turn, turned, sums, lift_in):
+    high, low = far_rows(got)
+    which = slot_turn[...][None]
+    for q in range(NQ):
+        h, l = high[q * MP : (q + 1) * MP], low[q * MP : (q + 1) * MP]
+        r = dot(w_rot[...], jnp.concatenate([h, l, h], axis=0).astype(BF16))
+        r = [tiles(r[o * MP : (o + 1) * MP]) for o in range(3)]
+        turned[q] = flat(jnp.where(which < 0.5, r[0], jnp.where(which < 1.5, r[1], r[2])))
+    for block in ((0, 1, 2), (3, 4, 5), (6, 7, 8)):
+        totals = [None] * len(block)
+        for q in range(NQ):
+            x = tiles(turned[q])
+            for i, p in enumerate(block):
+                term = x * slot_flux[q * NQ + p][None]
+                totals[i] = term if totals[i] is None else totals[i] + term
+        for i, p in enumerate(block):
+            sums[p * MP : (p + 1) * MP, :] = flat(totals[i])
+    high, low = halves(sums[...])
+    both = jnp.concatenate([high, low], axis=0).astype(BF16)
+    back = dot(both, picks[LANES : LANES + 2 * NE, :])
+    for f in range(NF):
+        c = slice(f * NE, (f + 1) * NE)
+        for p in range(NQ):
+            h = back[p * MP : (p + 1) * MP, c]
+            l = back[ROWS + p * MP : ROWS + (p + 1) * MP, c]
+            lift_in[f * 3 * MP : (f + 1) * 3 * MP, p * NE : (p + 1) * NE] = jnp.concatenate(
+                [h, l, h], axis=0
+            ).astype(BF16)
+    return dot(w_lift[...], lift_in[...])
 
 
 def turn(picked, w_rot, orient, q):
@@ -346,7 +407,14 @@
     table_two,
     picked,
     near,
-    lifts,
+    moved,
+    rows,
+    lines,
+    slot_flux,
+    slot_turn,
+    turned,
+    sums,
+    far_in,
     lift_in,
     send_a,
     send_b,
@@ -356,6 +424,7 @@
     recv_b,
     recv_c,
     recv_d,
+    kept,
     send_sem,
     recv_sem,
     n_dom,
@@ -429,13 +498,8 @@
 
             @pl.when(links[t][0])
             def _():
-                copy(stage, t).wait_send()
                 arrival(stage, t).wait_recv()
 
-    loads["stiff"].wait()
-    prepare_derive(stiff, w_der)
-    loads["jac"].wait()
-    spread_jacobians(jac, jac_wide)
     for t in range(4):
 
         @pl.when(jnp.logical_not(links[t][0]))
@@ -443,27 +507,32 @@
             recvs[t][...] = jnp.zeros_like(recvs[t])
 
     mats = (mats_a, mats_b)
-    loads["state"].wait()
-    predict(state, w_der, jac_wide, mats, first, second)
-    loads["proj"].wait()
+    for name in ("stiff", "state", "jac", "proj", "send_map"):
+        loads[name].wait()
+    prepare_derive(stiff, w_der)
+    spread_jacobians(jac, jac_wide)
     prepare_faces(proj, w_proj, padded)
-    loads["send_map"].wait()
     pack_columns(send_map, spare, packs)
-    project(lambda p: first[p], w_proj, table_one)
+
+    def project_one(block):
+        project([first[p] for p in block], block, w_proj, table_one)
+
+    predict(state, w_der, jac_wide, mats, first, kept, project_one)
     both = pick_local(table_one, picks, packs, [s.at[0] for s in sends], picked)
     peers = sum(there.astype(jnp.int32) for there, _, _ in links)
     pl.semaphore_wait(barrier, peers)
     start(0)
     for name in ("flux", "slot", "rot", "orient", "cluster", "stress"):
         loads[name].wait()
+    later(state, kept, second)
     prepare_volume(stiff, w_vol)
     pick_columns(slot, picks)
     spread_flux(flux, flux_wide)
     w_lift[...] = split_lift(padded[...])
     prepare_turn(rot, w_rot, padded_rot)
+    prepare_slots(flux, orient, picks, rows, lines, slot_flux, slot_turn)
     picked[...] = dot(both, picks[0:LANES, :])
     fine = jnp.broadcast_to(cluster[...], (NB, NE)) == 0
-    fine_face = jnp.broadcast_to(cluster[...], (MP, NE)) == 0
 
     def volume(field, base, target):
         for block in BLOCKS:
@@ -472,64 +541,60 @@
             for p, x in zip(block, mix(mats_a, jac_wide, block)):
                 target[p] = base(p) + x
 
-    def own_flux(face):
-        for f in range(NF):
-            totals = flux_term(lambda q: face(q, f), flux_wide, 0, f, None)
-            for p in range(NQ):
-                lifts[f * NQ + p] = flat(totals[p])
-
-    def near_flux():
+    def local_update(table, target):
+        for q in range(NQ):
+            for f, x in enumerate(turn(picked, w_rot, orient, q)):
+                near[q, f] = x
         for f in range(NF):
             totals = flux_term(
-                lambda q: near[q, f],
-                flux_wide,
-                1,
-                f,
-                [tiles(lifts[f * NQ + p]) for p in range(NQ)],
+                lambda q: table[q * MP : (q + 1) * MP, f * NE : (f + 1) * NE], flux_wide, 0, f, None
             )
+            totals = flux_term(lambda q: near[q, f], flux_wide, 1, f, totals)
             for p in range(NQ):
                 lift_in[f * 3 * MP : (f + 1) * 3 * MP, p * NE : (p + 1) * NE] = split_rows(
                     flat(totals[p])
                 )
-
-    def own_one(q, f):
-        return table_one[q * MP : (q + 1) * MP, f * NE : (f + 1) * NE]
-
-    def own_two(q, f):
-        late = table_two[q * MP : (q + 1) * MP, f * NE : (f + 1) * NE]
-        return jnp.where(fine_face, late, own_one(q, f) + late)
-
-    volume(lambda p: first[p], lambda p: state[p], middle)
-    own_flux(own_one)
+        lifted = dot(w_lift[...], lift_in[...])
+        for p in range(NQ):
+            target[p] = target[p] - lifted[:, p * NE : (p + 1) * NE]
+
+    def from_far(stage):
+        return far_update(
+            [r.at[stage] for r in recvs],
+            w_rot,
+            w_lift,
+            picks,
+            slot_flux,
+            slot_turn,
+            turned,
+            sums,
+            far_in,
+        )
+
+    volume(lambda p: first[p], lambda p: state[p], moved)
+    local_update(table_one, moved)
     finish(0)
-    pick_far([r.at[0] for r in recvs], picks, picked)
-    for q in range(NQ):
-        for f, x in enumerate(turn(picked, w_rot, orient, q)):
-            near[q, f] = x
-    near_flux()
-    lifted = dot(w_lift[...], lift_in[...])
+    lifted = from_far(0)
     for p in range(NQ):
-        middle[p] = jnp.where(fine, middle[p] - lifted[:, p * NE : (p + 1) * NE], state[p])
-
-    predict(middle, w_der, jac_wide, mats, fine_first, None)
-    project(lambda p: jnp.where(fine, fine_first[p], second[p]), w_proj, table_two)
+        x = moved[p] - lifted[:, p * NE : (p + 1) * NE]
+        moved[p] = x
+        middle[p] = jnp.where(fine, x, state[p])
+
+    def project_two(block):
+        late = [jnp.where(fine, fine_first[p], second[p]) for p in block]
+        for p, x in zip(block, late):
+            second[p] = x
+        project(late, block, w_proj, table_two)
+
+    predict(middle, w_der, jac_wide, mats, fine_first, None, project_two)
     both = pick_local(table_two, picks, packs, [s.at[1] for s in sends], picked)
     start(1)
     picked[...] = dot(both, picks[0:LANES, :])
-    volume(
-        lambda p: jnp.where(fine, fine_first[p], first[p] + second[p]),
-        lambda p: middle[p],
-        middle,
-    )
-    own_flux(own_two)
+    volume(lambda p: second[p], lambda p: moved[p], moved)
+    local_update(table_two, moved)
     finish(1)
-    pick_far([r.at[1] for r in recvs], picks, picked)
-    for q in range(NQ):
-        for f, x in enumerate(turn(picked, w_rot, orient, q)):
-            near[q, f] = jnp.where(fine_face, x, near[q, f] + x)
-    near_flux()
-    lifted = dot(w_lift[...], lift_in[...])
-    stepped = [middle[p] - lifted[:, p * NE : (p + 1) * NE] for p in range(NQ)]
+    lifted = from_far(1)
+    stepped = [moved[p] - lifted[:, p * NE : (p + 1) * NE] for p in range(NQ)]
     mean = (stepped[0] + stepped[1] + stepped[2]) / 3.0
     spread = [stepped[p] - mean for p in range(3)]
     lead = [s[0:1] for s in spread] + [stepped[p][0:1] for p in range(3, 6)]
@@ -545,6 +610,12 @@
         out[p] = mean + scaling * spread[p]
         out[3 + p] = scaling * stepped[3 + p]
         out[6 + p] = stepped[6 + p]
+    for t in range(4):
+
+        @pl.when(links[t][0])
+        def _():
+            for stage in range(2):
+                copy(stage, t).wait_send()
 
 
 def on_device(n_dom, n_sub, modal_state, stiffness, jacobians, flux_solvers, projector, rotations, yield_stress, cluster, orient, neighbour_slot, send_map):
@@ -596,7 +667,14 @@
             pltpu.VMEM((ROWS, LANES), F32),
             pltpu.VMEM((2 * ROWS, LANES), F32),
             pltpu.VMEM((NQ, NF, MP, NE), F32),
-            pltpu.VMEM((NF * NQ, MP, NE), F32),
+            field,
+            pltpu.VMEM((88, LANES), F32),
+            pltpu.VMEM((8, LANES), F32),
+            pltpu.VMEM((NQ * NQ, 8, 2 * NE), F32),
+            pltpu.VMEM((8, 2 * NE), F32),
+            pltpu.VMEM((NQ, MP, 2 * NE), F32),
+            pltpu.VMEM((ROWS, 2 * NE), F32),
+            pltpu.VMEM((3 * NF * MP, NQ * NE), BF16),
             pltpu.VMEM((3 * NF * MP, NQ * NE), BF16),
             pltpu.VMEM((2, HALF, NE), F32),
             pltpu.VMEM((2, HALF, NE), F32),
@@ -606,6 +684,7 @@
             pltpu.VMEM((2, HALF, NE), F32),
             pltpu.VMEM((2, QUARTER, NE), F32),
             pltpu.VMEM((2, QUARTER, NE), F32),
+            pltpu.VMEM((ORDER - 1, NQ, NB, NE), F32),
             pltpu.SemaphoreType.DMA((2, 4)),
             pltpu.SemaphoreType.DMA((2, 4)),
         ],

time: 26.9 us -> 26.3 us (0.978)
  Pallas kernels: 26.1 us -> 25.4 us
    pallas_call x1, Pallas kernels: 26.1 us -> 25.4 us  [on_device(): pl.pallas_call(body, out_shape=jax.ShapeDtypeStruct((NQ, NB, NE), F32), i...]
where the time goes in v2:
time: 26.3 us; the launch traced here: 26.1 us
  Pallas kernels  25.4 us (97%)
  local copies, waits for them, and re-layouts  0.7 us (3%)
    pallas_call x1, Pallas kernels, on_device(): pl.pallas_call(body, out_shape=jax.ShapeDtypeStruct((NQ, NB, NE), F32), i...  25.4 us
    unnamed x1, local copies, waits for them, and re-layouts  0.7 us

profile of v2, /device:TPU:4, one launch (start us, length us, event | category | flops | bytes accessed | tf_op | source)
XLA Modules:
  0.0 26.1 jit_solution(17784928386377383733)
XLA Ops:
  0.0 25.4 %shard_map.109 = f32[9,56,128]{2,1,0:T(8,128)S(1)} custom-call(f32[9,56,128]{2,1,0:T(8,128)} %bitcast.10, f32[3,56,56]{2,1,0:T(8,128)} %refs_1_.1, f32[9,9,3,128]{3,2,1,0:T(4,128)} %bitcast.11, f32[2,9,9,4,128]{4,3,2,1,0:T(4,128)} %bitcast.9, f32[21,4,56]{2,1,0:T(4,128)} %bitcast.12, f32[3,21,21]{2,1,0:T(8,128)} %refs_5_.1, f32[1,128]{1,0:T(1,128)} %bitcast.14, ...), custom_call_target="tpu_custom_call" | custom-call | tf_op jit(solution)/shard_map/pallas_call | solution.py:630
  25.4 0.7 %copy.13 = f32[56,9,128]{2,0,1:T(8,128)} copy(f32[56,9,128]{2,0,1:T(8,128)S(1)} %bitcast.8) | data formatting | bytes 516096

commit v3 on v2

--- a/solution.py
+++ b/solution.py
@@ -147,32 +147,11 @@
 
 
 def pack_columns(send_map, spare, packs):
-    lane = iota((8, NE), 1)
-    first = jnp.broadcast_to(send_map[0:1, 0:NE], (8, NE))
-    turned = pltpu.roll(first, 64, 1)
-    spare[:, 0:64] = jnp.broadcast_to(send_map[0:1, NE : NE + 64], (8, 64))
-    second = spare[...]
-    by = [second] + [pltpu.roll(second, 32 * r, 1) for r in (1, 2, 3)]
-    group = (
-        (lane >= 32).astype(jnp.int32)
-        + (lane >= 64).astype(jnp.int32)
-        + (lane >= 96).astype(jnp.int32)
-    )
-
-    def four(a, b, c, d):
-        return jnp.where(
-            group == 0, a, jnp.where(group == 1, b, jnp.where(group == 2, c, d))
-        )
-
-    wants = [
-        jnp.where(lane < 64, first, turned),
-        jnp.where(lane < 64, turned, first),
-        four(by[0], by[1], by[2], by[3]),
-        four(by[3], by[0], by[1], by[2]),
-    ]
-    for t in range(4):
+    spare[...] = jnp.full((8, NE), -1, jnp.int32)
+    spare[0:1, 0:64] = send_map[0:1, NE : NE + 64]
+    for t, want in enumerate((send_map[0:1, 0:NE], spare[0:1, :])):
         packs[:, t * NE : (t + 1) * NE] = as_bf16(
-            iota((LANES, NE), 0) == jnp.broadcast_to(wants[t][0:1, :], (LANES, NE))
+            iota((LANES, NE), 0) == jnp.broadcast_to(want, (LANES, NE))
         )
 
 
@@ -238,22 +217,24 @@
             ]
 
 
-def pick_local(table, picks, packs, packed, picked):
+def pick_local(table, packs, packed):
     high, low = halves(table[...])
     both = jnp.concatenate([high, low], axis=0).astype(BF16)
     got = dot(both, packs[...])
     rows = got[0:ROWS] + got[ROWS : 2 * ROWS]
+    rows = jnp.concatenate([rows, jnp.zeros((256 - ROWS, 2 * NE), F32)], axis=0)
     lane = iota((HALF, NE), 1)
-    zeros = jnp.zeros((256 - ROWS, LANES), F32)
-    rows = jnp.concatenate([rows, zeros], axis=0)
+    top, bottom = rows[0:HALF, 0:NE], rows[HALF : 2 * HALF, 0:NE]
+    packed[0][...] = jnp.where(lane < 64, top, pltpu.roll(bottom, 64, 1))
+    packed[1][...] = jnp.where(lane < 64, pltpu.roll(top, 64, 1), bottom)
+    lane = iota((QUARTER, NE), 1)
+    parts = [rows[QUARTER * k : QUARTER * (k + 1), NE : 2 * NE] for k in range(4)]
     for t in range(2):
-        cols = slice(t * NE, (t + 1) * NE)
-        packed[t][...] = jnp.where(lane < 64, rows[0:HALF, cols], rows[HALF : 2 * HALF, cols])
-    lane = iota((QUARTER, NE), 1)
-    for t in range(2, 4):
-        cols = slice(t * NE, (t + 1) * NE)
-        g = [rows[QUARTER * k : QUARTER * (k + 1), cols] for k in range(4)]
-        packed[t][...] = jnp.where(
+        g = [
+            x if k == t else pltpu.roll(x, (32 * k - 32 * t) % 128, 1)
+            for k, x in enumerate(parts)
+        ]
+        packed[2 + t][...] = jnp.where(
             lane < 64, jnp.where(lane < 32, g[0], g[1]), jnp.where(lane < 96, g[2], g[3])
         )
     return both
@@ -518,7 +499,7 @@
         project([first[p] for p in block], block, w_proj, table_one)
 
     predict(state, w_der, jac_wide, mats, first, kept, project_one)
-    both = pick_local(table_one, picks, packs, [s.at[0] for s in sends], picked)
+    both = pick_local(table_one, packs, [s.at[0] for s in sends])
     peers = sum(there.astype(jnp.int32) for there, _, _ in links)
     pl.semaphore_wait(barrier, peers)
     start(0)
@@ -587,7 +568,7 @@
         project(late, block, w_proj, table_two)
 
     predict(middle, w_der, jac_wide, mats, fine_first, None, project_two)
-    both = pick_local(table_two, picks, packs, [s.at[1] for s in sends], picked)
+    both = pick_local(table_two, packs, [s.at[1] for s in sends])
     start(1)
     picked[...] = dot(both, picks[0:LANES, :])
     volume(lambda p: second[p], lambda p: moved[p], moved)
@@ -656,7 +637,7 @@
             pltpu.VMEM((2 * NF * NQ * NQ, 8, NE), F32),
             pltpu.VMEM((8, NE), jnp.int32),
             pltpu.VMEM((LANES + 2 * NE, LANES), BF16),
-            pltpu.VMEM((LANES, LANES), BF16),
+            pltpu.VMEM((LANES, 2 * NE), BF16),
             pltpu.VMEM((3 * NB, NQ * NE), F32),
             pltpu.VMEM((3 * NB, NQ * NE), F32),
             field,

time: 26.3 us -> 26.4 us (level)
  the two profiles are of different devices: /device:TPU:4 before, /device:TPU:2 now
where the time goes in v3:
time: 26.4 us; the launch traced here: 26.3 us
  Pallas kernels  25.5 us (97%)
  local copies, waits for them, and re-layouts  0.7 us (3%)
    pallas_call x1, Pallas kernels, on_device(): pl.pallas_call(body, out_shape=jax.ShapeDtypeStruct((NQ, NB, NE), F32), i...  25.5 us
    unnamed x1, local copies, waits for them, and re-layouts  0.7 us

profile of v3, /device:TPU:2, one launch (start us, length us, event | category | flops | bytes accessed | tf_op | source)
XLA Modules:
  0.0 26.3 jit_solution(11704487754476465878)
XLA Ops:
  0.0 25.5 %shard_map.109 = f32[9,56,128]{2,1,0:T(8,128)S(1)} custom-call(f32[9,56,128]{2,1,0:T(8,128)} %bitcast.10, f32[3,56,56]{2,1,0:T(8,128)} %refs_1_.1, f32[9,9,3,128]{3,2,1,0:T(4,128)} %bitcast.11, f32[2,9,9,4,128]{4,3,2,1,0:T(4,128)} %bitcast.9, f32[21,4,56]{2,1,0:T(4,128)} %bitcast.12, f32[3,21,21]{2,1,0:T(8,128)} %refs_5_.1, f32[1,128]{1,0:T(1,128)} %bitcast.14, ...), custom_call_target="tpu_custom_call" | custom-call | tf_op jit(solution)/shard_map/pallas_call | solution.py:611
  25.6 0.7 %copy.13 = f32[56,9,128]{2,0,1:T(8,128)} copy(f32[56,9,128]{2,0,1:T(8,128)S(1)} %bitcast.8) | data formatting | bytes 516096
